TPU v7x, 32 devices: a whole 2x2x4 slice. The times are simulated.
32 devices in a mesh: group: 16 (over z, y, core), tp: 2 (over x).
Axes of the slice: x: 2, y: 2, z: 4, core: 2. Of those that a mesh axis runs over, the one named last changes fastest.
Arguments:
- tokens: bfloat16 [8192, 3200], P('group', 'tp'), may hold values from -6 to 6
- norm_gain: bfloat16 [3200], P('tp'), may hold values from 0.25 to 1.75
- w_qkv: bfloat16 [3200, 3, 2048], P('group', None, 'tp'), may hold values from -1 to 1, as said below
- qk_gain: float32 [2, 2048], P(None, 'tp'), may hold values from 0.5 to 8
- w_out: bfloat16 [2048, 3200], P('tp', 'group'), may hold values from -0.125 to 0.125
- layer_scale: float32 [3200], P('tp'), may hold values from 0.3 to 1.5
- request: int32 [8192], P('group'), may hold values from 0 to 8191, as said below
- owner: int32 [8192, 1], P('group'), may hold values from 0 to 15; in each aligned block of 512 rows (0 to 511, 512 to 1023, ...) at most 64 rows name the same one
Outputs:
- routed: bfloat16 [16, 16, 64, 3200], P('group', None, None, 'tp')
Inputs may be any that keep to these rules, and one draw needn't show every extreme that they name: Requests never cross a block of 1024 rows starting at a multiple of 1024, and blocks share none; in each such block exactly one request holds rows on both sides of its middle, at most 128 on each side, exactly 128 on each side in the first block; the first row's number is 0 and the last row's is 8191. Among one group's 512 rows at most 64 name the same owner; some owner is named by exactly 64 rows of some group. `w_qkv`: column scales of the projections vary across the columns.
All inputs are finite; a program needn't handle non-finite values.
Results may differ from a plain program's by a relative error of at most 0.0117.
The roundings to bfloat16 on the way count: a program that leaves them out, or rounds other values in their place, can miss the bound.
Values may be sent and summed in bfloat16 or wider, within the bound.
A program may use at most 128 MiB of HBM per device.

v0:
```python
import math
import jax
import jax.numpy as jnp
from jax import lax
from jax.sharding import PartitionSpec as P

HD = 128
SHARE = 128


def swapped(value, axis, apart):
    mask = 2**apart
    pairs = [(source, source ^ mask) for source in range(lax.axis_size(axis))]
    return lax.ppermute(value, axis, pairs)


def shards(tokens, norm_gain, w_qkv, qk_gain, w_out, layer_scale, request, owner):
    rows = tokens.shape[0]
    feat_local = tokens.shape[1]
    tp_count = lax.axis_size("tp")
    group_count = lax.axis_size("group")
    local_width = w_qkv.shape[2]
    head_count = local_width // HD
    whole, gain_all = (
        lax.all_gather(tokens, "tp", axis=1, tiled=True),
        lax.all_gather(norm_gain.reshape(1, feat_local), "tp", axis=1, tiled=True),
    )
    xwide = whole.astype(jnp.float32)
    stat = jnp.mean(xwide * xwide, axis=-1, keepdims=True)
    normed = (xwide * lax.rsqrt(stat + 1e-06) * gain_all.astype(jnp.float32)).astype(jnp.bfloat16)
    piece = lax.all_gather(w_qkv, "group", axis=0, tiled=True)
    qkv = jnp.dot(
        normed, piece.reshape(piece.shape[0], 3 * local_width), preferred_element_type=jnp.float32
    ).reshape(rows, 3, local_width)
    query = qkv[:, 0, :]
    key_rows = qkv[:, 1, :]
    value = qkv[:, 2, :].astype(jnp.bfloat16)
    qsum, ksum = lax.psum(
        (jnp.sum(query * query, axis=-1), jnp.sum(key_rows * key_rows, axis=-1)), "tp"
    )
    total_width = local_width * tp_count
    qnorm = (query * lax.rsqrt(qsum / total_width + 1e-06)[:, None] * qk_gain[0]).astype(
        jnp.bfloat16
    )
    knorm = (key_rows * lax.rsqrt(ksum / total_width + 1e-06)[:, None] * qk_gain[1]).astype(
        jnp.bfloat16
    )
    parity = lax.axis_index("group") % 2
    seam = jnp.where(parity == 0, rows - SHARE, 0).astype(jnp.int32)
    key_window = lax.dynamic_slice_in_dim(knorm, seam, SHARE, 0)
    value_window = lax.dynamic_slice_in_dim(value, seam, SHARE, 0)
    id_window = lax.dynamic_slice_in_dim(request, seam, SHARE, 0)
    paired, paired_ids = swapped((jnp.stack([key_window, value_window]), id_window), "group", 0)
    all_keys = jnp.concatenate([knorm, paired[0]], axis=0)
    all_values = jnp.concatenate([value, paired[1]], axis=0)
    all_ids = jnp.concatenate([request, paired_ids], axis=0)
    qheads = qnorm.reshape(rows, head_count, HD)
    kheads = all_keys.reshape(rows + SHARE, head_count, HD)
    vheads = all_values.reshape(rows + SHARE, head_count, HD)
    scores = jnp.einsum(
        "qhd,khd->hqk", qheads, kheads, preferred_element_type=jnp.float32
    ) / math.sqrt(HD)
    same = request[:, None] == all_ids[None, :]
    scores = jnp.where(same[None], scores, -jnp.inf)
    top = jnp.max(scores, axis=-1, keepdims=True)
    expo = jnp.exp(scores - top)
    probs = (expo / jnp.sum(expo, axis=-1, keepdims=True)).astype(jnp.bfloat16)
    attended = jnp.einsum("hqk,khd->qhd", probs, vheads, preferred_element_type=jnp.float32)
    attended = attended.astype(jnp.bfloat16).reshape(rows, local_width)
    partial_terms = jnp.dot(
        attended,
        lax.all_gather(w_out, "group", axis=1, tiled=True),
        preferred_element_type=jnp.float32,
    )
    mine = lax.psum_scatter(
        partial_terms.astype(jnp.bfloat16), "tp", scatter_dimension=1, tiled=True
    ).astype(jnp.float32)
    mixed = (tokens.astype(jnp.float32) + layer_scale * mine).astype(jnp.bfloat16)
    capacity = max(2, 2 * rows // group_count)
    target = owner[:, 0]
    onehot = (target[:, None] == jnp.arange(group_count, dtype=jnp.int32)[None, :]).astype(
        jnp.int32
    )
    slot = jnp.sum((jnp.cumsum(onehot, axis=0) - onehot) * onehot, axis=-1)
    outbox = (
        jnp.zeros((group_count, capacity, feat_local), jnp.bfloat16).at[target, slot].set(mixed)
    )
    inbox = lax.all_to_all(outbox, "group", split_axis=0, concat_axis=0, tiled=True)
    return inbox[None]


def solution(mesh):
    in_specs = (
        P("group", "tp"),
        P("tp"),
        P("group", None, "tp"),
        P(None, "tp"),
        P("tp", "group"),
        P("tp"),
        P("group"),
        P("group", None),
    )
    out_specs = P("group", None, None, "tp")
    return jax.shard_map(shards, mesh=mesh, in_specs=in_specs, out_specs=out_specs, check_vma=False)
```

profile of v0, /device:TPU:1, one launch (start us, length us, event | category | flops | bytes accessed | tf_op | source)
XLA Modules:
  0.0 463.0 jit_solution(18097618292027908334)
XLA Ops:
  6.6 0.7 all-gather.5.cloned.1.call-update
  7.3 0.0 all-gather.7.cloned.1.call-start
  7.3 0.7 all-gather.7.cloned.1.call-update
  8.1 0.7 all-gather.9.cloned.1.call-update
  8.8 0.0 reduce-scatter.2.cloned.1.call-start
  8.8 0.1 dynamic_slice.11
  8.9 0.1 collective-permute-start.1
  9.0 0.6 dynamic-slice.1
  10.2 0.3 dynamic-update-slice
  10.5 5.0 %all-reduce = bf16[3200]{0:T(1024)(128)(2,1)S(1)} all-reduce(bf16[3200]{0:T(1024)(128)(2,1)S(1)} %dynamic-update-slice), channel_id=2, replica_groups=mesh['group'=16,'tp'=2] {'tp'}, use_global_device_ids=true, to_apply=%add | all-reduce | flops 3200 | bytes 12800
  15.6 1.0 broadcast_compare_fusion
  16.6 40.9 %all-gather.5.cloned.1.call-done = bf16[512,3200]{0,1:T(8,128)(2,1)} async-done(((bf16[512,1600]{0,1:T(8,128)(2,1)}), bf16[512,3200]{0,1:T(8,128)(2,1)}) %all-gather.5.cloned.1.call-update) | async-done | bytes 3276816 | tf_op jit(solution)/shard_map/all_gather | solution.py:25
  57.4 2.7 fusion.4
  60.1 101.9 %all-gather.7.cloned.1.call-done = bf16[3200,3,1024]{2,0,1:T(8,128)(2,1)} async-done(((bf16[200,3,1024]{2,0,1:T(8,128)(2,1)}), bf16[3200,3,1024]{2,0,1:T(8,128)(2,1)}) %all-gather.7.cloned.1.call-update) | async-done | bytes 19660816 | tf_op jit(solution)/shard_map/all_gather | solution.py:31
  162.1 24.0 %copy.25 = bf16[3200,3,1024]{0,2,1:T(8,128)(2,1)} copy(bf16[3200,3,1024]{2,0,1:T(8,128)(2,1)} %all-gather.7.cloned.1.call-done) | data formatting | bytes 39321600 | tf_op jit(solution)/shard_map/all_gather | solution.py:31
  186.0 17.9 %fusion.1 = f32[512,3,1024]{2,0,1:T(8,128)} fusion(bf16[3200,3,1024]{0,2,1:T(8,128)(2,1)} %copy.25, bf16[512,3200]{0,1:T(8,128)(2,1)S(1)} %copy-done.2, f32[3200]{0:T(1024)S(1)} %mul.120, f32[512]{0:T(512)S(1)} %add_rsqrt_fusion.2), kind=kOutput, calls=%fused_computation.2 | convolution fusion | flops 10072883200 | bytes 29243904 | tf_op jit(solution)/shard_map/dot_general | solution.py:32
  203.9 1.7 slice.52
  205.7 5.1 %slice_bitcast_fusion = (f32[64,8,8,128]{3,1,2,0:T(8,128)S(1)}, f32[64,8,8,128]{3,1,2,0:T(8,128)}, f32[512]{0:T(512)S(1)}, f32[512,1024]{1,0:T(8,128)}) fusion(f32[512,3,1024]{2,0,1:T(8,128)} %fusion.1), kind=kLoop, calls=%fused_computation.31 | loop fusion | flops 1048064 | bytes 10487808
  210.7 0.5 copy.38
  211.2 1.8 multiply_reduce_fusion.1
  213.0 4.0 all-reduce.1
  217.0 0.1 dynamic-slice.2
  217.0 1.3 copy.36
  218.4 1.3 fusion.32
  219.7 0.1 pad_maximum_fusion
  219.8 1.5 collective-permute-start
  221.3 0.5 copy.39
  221.8 0.5 fusion.16
  222.3 0.5 collective-permute-done
  222.8 0.7 fusion.42
  223.6 1.8 copy.27
  225.3 0.8 copy.31
  226.2 1.1 copy.32
  227.3 5.4 %fusion.23 = f32[8,512,640]{2,1,0:T(8,128)} fusion(bf16[128,8,128]{2,0,1:T(8,128)(2,1)S(1)} %copy.32, bf16[512,8,128]{2,0,1:T(8,128)(2,1)S(1)} %fusion.16, f32[512,8,128]{2,1,0:T(8,128)S(1)} %bitcast.68, f32[8,128]{1,0:T(8,128)S(1)} %bitcast.76, f32[512]{0:T(512)S(1)} %add_rsqrt_fusion), kind=kOutput, calls=%fused_computation.38 | convolution fusion | flops 675282944 | bytes 13899776 | tf_op jit(solution)/shard_map/qhd,khd->hqk/dot_general | solution.py:60
  232.8 15.3 %fusion.44 = (f32[8,512]{1,0:T(8,128)S(1)}, f32[8,512,640]{2,1,0:T(8,128)}) fusion(f32[8,512,640]{2,1,0:T(8,128)} %fusion.23, pred[512,640]{1,0:T(8,128)(4,1)S(1)} %copy-done.4), kind=kOutput, calls=%fused_computation.76 | output fusion | flops 15729279 | bytes 21315584 | tf_op jit(solution)/shard_map/sub | solution.py:66
  248.1 5.9 %fusion.19 = bf16[8,128,512]{2,1,0:T(8,128)(2,1)S(1)} fusion(f32[8,512,640]{2,1,0:T(8,128)} %get-tuple-element.16, f32[8,512]{1,0:T(8,128)S(1)} %get-tuple-element.15, bf16[128,8,128]{0,2,1:T(8,128)(2,1)S(1)} %bitcast.71, bf16[512,8,128]{0,2,1:T(8,128)(2,1)S(1)} %bitcast.69), kind=kOutput, calls=%fused_computation.34 | convolution fusion | flops 679477248 | bytes 12861440 | tf_op jit(solution)/shard_map/hqk,khd->qhd/dot_general | solution.py:68
  254.1 7.8 %convolution_convert_fusion = bf16[512,3200]{0,1:T(8,128)(2,1)} fusion(bf16[1024,3200]{0,1:T(8,128)(2,1)} %all-gather.9.cloned.1.call-done, bf16[512,1024]{0,1:T(8,128)(2,1)S(1)} %bitcast.78), kind=kOutput, calls=%fused_computation.13 | convolution fusion | flops 3357081600 | bytes 10878976 | tf_op jit(solution)/shard_map/dot_general | solution.py:70
  261.9 0.7 copy-done.6
  262.5 1.3 reduce-window.6
  263.9 0.2 slice_reduce_fusion
  264.1 0.1 fusion.35
  264.3 42.3 %reduce-scatter.2.cloned.1.call-done = bf16[512,1600]{0,1:T(8,128)(2,1)} async-done(((bf16[512,3200]{0,1:T(8,128)(2,1)}), bf16[512,1600]{0,1:T(8,128)(2,1)}) %reduce-scatter.2.cloned.1.call-update) | async-done | bytes 1638416 | tf_op jit(solution)/shard_map/reduce_scatter | solution.py:75
  306.6 2.0 add_convert_fusion
  308.6 2.3 copy.33
  310.9 0.4 broadcast_in_dim.16
  311.3 60.7 %scatter_fusion = bf16[16,64,1600]{2,1,0:T(8,128)(2,1)S(1)} fusion(bf16[16,64,1600]{2,1,0:T(8,128)(2,1)S(1)} %broadcast_in_dim.16, s32[512]{0:T(512)S(1)} %bitcast.65, bf16[512,1600]{1,0:T(8,128)(2,1)} %copy.33), kind=kCustom, calls=%fused_computation | custom fusion | bytes 4919296 | tf_op jit(solution)/shard_map/scatter | solution.py:86
  372.0 82.8 %all_to_all.5 = bf16[16,64,1600]{2,1,0:T(8,128)(2,1)S(1)} all-to-all(bf16[16,64,1600]{2,1,0:T(8,128)(2,1)S(1)} %scatter_fusion), channel_id=1, replica_groups=mesh['group'=16,'tp'=2] {'group'}, dimensions={0} | all-to-all | bytes 6553600 | tf_op jit(solution)/shard_map/all_to_all | solution.py:88
  454.8 1.8 copy.55
  (40 shorter events, 0.3 us)
Async XLA Ops:
  6.5 2.4 copy-start.11
  6.5 2.3 copy-start.8
  6.5 3.7 copy-start.10
  6.5 4.0 copy-start.9
  6.5 50.9 %all-gather.5.cloned.1.call-start = ((), (), s32[]{:S(2)}) async-start(), calls=%async_computation.2 | async-start | bytes 4915200 | tf_op jit(solution)/shard_map/all_gather | solution.py:25
  7.3 154.8 %all-gather.7.cloned.1.call-start = ((), (), s32[]{:S(2)}) async-start(), calls=%async_computation.3 | async-start | bytes 20889600 | tf_op jit(solution)/shard_map/all_gather | solution.py:31
  8.0 246.0 %all-gather.9.cloned.1.call-start = ((), (), s32[]{:S(2)}) async-start(), calls=%async_computation.4 | async-start | bytes 6963200 | tf_op jit(solution)/shard_map/all_gather | solution.py:72
  8.8 297.8 %reduce-scatter.2.cloned.1.call-start = ((), (), s32[]{:S(2)}) async-start(), calls=%async_computation.5 | async-start | bytes 4915200 | tf_op jit(solution)/shard_map/reduce_scatter | solution.py:75
  8.9 6.7 %collective-permute-start.1 = (s32[128]{0:T(128)S(1)}, s32[128]{0:T(128)S(1)}, u32[]{:S(2)}, u32[]{:S(2)}) collective-permute-start(s32[128]{0:T(128)S(1)} %dynamic_slice.11), channel_id=1, source_target_pairs={{0,2},{2,0},{4,6},{6,4},{8,10},{10,8},{12,14},{14,12},{16,18},{18,... | collective-permute-start | bytes 1544 | tf_op jit(solution)/shard_map/ppermute | solution.py:14
  60.1 125.9 %copy-start.2 = (bf16[512,3200]{0,1:T(8,128)(2,1)S(1)}, bf16[512,3200]{0,1:T(8,128)(2,1)}, u32[]{:S(2)}) copy-start(bf16[512,3200]{0,1:T(8,128)(2,1)} %all-gather.5.cloned.1.call-done) | copy-start | bytes 9830404
  218.4 2.9 copy-start
  219.8 3.0 collective-permute-start
  227.3 5.4 %copy-start.4 = (pred[512,640]{1,0:T(8,128)(4,1)S(1)}, pred[512,640]{1,0:T(8,128)(4,1)}, u32[]{:S(2)}) copy-start(pred[512,640]{1,0:T(8,128)(4,1)} %broadcast_compare_fusion) | copy-start | bytes 983044
  232.7 15.3 %copy-start.3 = (bf16[512,1,1024]{0,2,1:T(8,128)(2,1)S(1)}, bf16[512,1,1024]{0,2,1:T(8,128)(2,1)}, u32[]{:S(2)}) copy-start(bf16[512,1,1024]{0,2,1:T(8,128)(2,1)} %copy.36) | copy-start | bytes 3145732
  232.7 15.3 %copy-start.5 = (bf16[1,128,1024]{1,2,0:T(8,128)(2,1)S(1)}, bf16[1,128,1024]{1,2,0:T(8,128)(2,1)}, u32[]{:S(2)}) copy-start(bf16[1,128,1024]{1,2,0:T(8,128)(2,1)} %copy.27) | copy-start | bytes 786436
  261.8 0.7 copy-start.6
  261.8 44.7 %copy-start.1 = (bf16[512,1600]{0,1:T(8,128)(2,1)S(1)}, bf16[512,1600]{0,1:T(8,128)(2,1)}, u32[]{:S(2)}) copy-start(bf16[512,1600]{0,1:T(8,128)(2,1)} %param.8) | copy-start | bytes 4915204
  261.9 44.7 %copy-start.7 = (f32[1600]{0:T(1024)S(1)}, f32[1600]{0:T(1024)}, u32[]{:S(2)}) copy-start(f32[1600]{0:T(1024)} %param.13) | copy-start | bytes 19204
Sparse Core Ops, SparseCore 0:
  8.9 48.4 all-gather.4
  59.0 103.0 all-gather.6
  164.4 63.3 all-gather.8
  262.0 44.5 reduce-scatter.1
where the time goes:
time: 466 us; the launch traced here: 463 us
  waiting for transfers between devices  188 us (40%)
  local copies, waits for them, and re-layouts  99.5 us (21%)
  blocking collectives  91.8 us (20%)
  matrix products  37 us (8%)
  other arithmetic  31.2 us (7%)
  between operations  14 us (3%)
    all_gather x1, waiting for transfers between devices, shards(): piece = lax.all_gather(w_qkv, 'group', axis=0, tiled=True)  102 us
    all_to_all x1, blocking collectives, shards(): lax.all_to_all(outbox, 'group', split_axis=0, concat_axis=0, tiled=True)  82.8 us
    scatter x1, local copies, waits for them, and re-layouts, shards(): jnp.zeros((group_count, capacity, feat_local), jnp.bfloat16)  60.7 us
    reduce_scatter x1, waiting for transfers between devices, shards(): lax.psum_scatter(partial_terms.astype(jnp.bfloat16), 'tp', scatter_dimens...  42.3 us
    all_gather x1, waiting for transfers between devices, shards(): lax.all_gather(tokens, 'tp', axis=1, tiled=True)  40.9 us
    all_gather x1, local copies, waits for them, and re-layouts, shards(): piece = lax.all_gather(w_qkv, 'group', axis=0, tiled=True)  24 us
    dot_general x1, matrix products, shards(): jnp.dot(normed, piece.reshape(piece.shape[0], 3 * local_width), preferred...  17.9 us
    sub x1, other arithmetic, shards(): expo = jnp.exp(scores - top)  15.3 us
  transfers between devices with their start and end apart: 6, of which 4 were waited for; matrix products, arithmetic and copies ran while one was open for 20% of the time, Pallas kernels for 0%

commit v1 on v0

--- a/solution.py
+++ b/solution.py
@@ -28,7 +28,24 @@
     xwide = whole.astype(jnp.float32)
     stat = jnp.mean(xwide * xwide, axis=-1, keepdims=True)
     normed = (xwide * lax.rsqrt(stat + 1e-06) * gain_all.astype(jnp.float32)).astype(jnp.bfloat16)
-    piece = lax.all_gather(w_qkv, "group", axis=0, tiled=True)
+    devices, index, width = (lax.axis_size("group"), lax.axis_index("group"), w_qkv.shape[0])
+    forward = [(i, (i + 1) % devices) for i in range(devices)]
+    behind = [(i, (i - 1) % devices) for i in range(devices)]
+    whole_2 = jnp.zeros((*w_qkv.shape[:0], devices * width, *w_qkv.shape[0 + 1 :]), w_qkv.dtype)
+    whole_2 = lax.dynamic_update_slice_in_dim(whole_2, w_qkv, index * width, axis=0)
+    from_left = from_right = w_qkv
+    middle = devices // 2
+    for hop in range(1, middle + 1):
+        from_left = lax.ppermute(from_left, "group", forward)
+        whole_2 = lax.dynamic_update_slice_in_dim(
+            whole_2, from_left, (index - hop) % devices * width, axis=0
+        )
+        if hop < devices - middle:
+            from_right = lax.ppermute(from_right, "group", behind)
+            whole_2 = lax.dynamic_update_slice_in_dim(
+                whole_2, from_right, (index + hop) % devices * width, axis=0
+            )
+    piece = whole_2
     qkv = jnp.dot(
         normed, piece.reshape(piece.shape[0], 3 * local_width), preferred_element_type=jnp.float32
     ).reshape(rows, 3, local_width)

time: 466 us -> 827 us (1.77)
  local copies, waits for them, and re-layouts: 99.5 us -> 372 us
  waiting for transfers between devices: 188 us -> 247 us
  starting transfers between devices: 1.72 us -> 23 us
    dynamic_update_slice x0 -> x16, local copies, waits for them, and re-layouts: none -> 264 us  [the longest x8 131 us: shards(): lax.dynamic_update_slice_in_dim(whole_2, from_left, (index - hop) % devic...]
    ppermute x0 -> x15, waiting for transfers between devices: none -> 206 us  [the longest x8 123 us: shards(): from_left = lax.ppermute(from_left, 'group', forward)]
    all_gather x1 -> x0, waiting for transfers between devices: 102 us -> none  [shards(): piece = lax.all_gather(w_qkv, 'group', axis=0, tiled=True)]
    all_gather x1, waiting for transfers between devices: 40.9 us -> 0.01 us  [shards(): lax.all_gather(tokens, 'tp', axis=1, tiled=True)]
    all_gather x1 -> x0, local copies, waits for them, and re-layouts: 24 us -> none  [shards(): piece = lax.all_gather(w_qkv, 'group', axis=0, tiled=True)]
    ppermute x0 -> x15, local copies, waits for them, and re-layouts: none -> 20.6 us  [the longest x8 12 us: shards(): from_left = lax.ppermute(from_left, 'group', forward)]
    ppermute x0 -> x15, starting transfers between devices: none -> 20.1 us  [the longest x8 20 us: shards(): from_left = lax.ppermute(from_left, 'group', forward)]
  transfers between devices with their start and end apart: 6 -> 20, of which waited for: 4 -> 14; matrix products, arithmetic and copies ran while one was open for 20% -> 44% of each run, Pallas kernels for 0% -> 0%
where the time goes in v1:
time: 827 us; the launch traced here: 816 us
  local copies, waits for them, and re-layouts  372 us (45%)
  waiting for transfers between devices  247 us (30%)
  blocking collectives  90.7 us (11%)
  matrix products  38 us (5%)
  other arithmetic  30.7 us (4%)
  starting transfers between devices  23 us (3%)
  between operations  14.7 us (2%)
    dynamic_update_slice x8, local copies, waits for them, and re-layouts, shards(): lax.dynamic_update_slice_in_dim(whole_2, from_left, (index - hop) % devic...  131 us
    ppermute x8, waiting for transfers between devices, shards(): from_left = lax.ppermute(from_left, 'group', forward)  123 us
    dynamic_update_slice x7, local copies, waits for them, and re-layouts, shards(): lax.dynamic_update_slice_in_dim(whole_2, from_right, (index + hop) % devi...  117 us
    all_to_all x1, blocking collectives, shards(): lax.all_to_all(outbox, 'group', split_axis=0, concat_axis=0, tiled=True)  82.8 us
    ppermute x7, waiting for transfers between devices, shards(): from_right = lax.ppermute(from_right, 'group', behind)  82.2 us
    scatter x1, local copies, waits for them, and re-layouts, shards(): jnp.zeros((group_count, capacity, feat_local), jnp.bfloat16)  60.7 us
    reduce_scatter x1, waiting for transfers between devices, shards(): lax.psum_scatter(partial_terms.astype(jnp.bfloat16), 'tp', scatter_dimens...  41.1 us
    ppermute x8, starting transfers between devices, shards(): from_left = lax.ppermute(from_left, 'group', forward)  20 us
  transfers between devices with their start and end apart: 20, of which 14 were waited for; matrix products, arithmetic and copies ran while one was open for 44% of the time, Pallas kernels for 0%

profile of v1, /device:TPU:1, one launch (start us, length us, event | category | flops | bytes accessed | tf_op | source)
XLA Modules:
  0.0 815.9 jit_solution(14622143040544029255)
XLA Ops:
  6.6 2.7 collective-permute-start
  9.3 27.2 %collective-permute-done = bf16[200,3,1024]{2,0,1:T(8,128)(2,1)} collective-permute-done((bf16[200,3,1024]{2,0,1:T(8,128)(2,1)}, bf16[200,3,1024]{2,0,1:T(8,128)(2,1)}, u32[]{:S(2)}, u32[]{:S(2)}) %collective-permute-start) | collective-permute-done | bytes 1228832 | tf_op jit(solution)/shard_map/ppermute | solution.py:39
  36.4 2.5 collective-permute-start.2
  39.0 13.4 %collective-permute-done.1 = bf16[200,3,1024]{2,0,1:T(8,128)(2,1)S(1)} collective-permute-done((bf16[200,3,1024]{2,0,1:T(8,128)(2,1)}, bf16[200,3,1024]{2,0,1:T(8,128)(2,1)S(1)}, u32[]{:S(2)}, u32[]{:S(2)}) %collective-permute-start.1) | collective-permute-done | bytes 1228832 | tf_op jit(solution)/shard_map/ppermute | solution.py:44
  52.4 12.9 %collective-permute-done.2 = bf16[200,3,1024]{2,0,1:T(8,128)(2,1)} collective-permute-done((bf16[200,3,1024]{2,0,1:T(8,128)(2,1)}, bf16[200,3,1024]{2,0,1:T(8,128)(2,1)}, u32[]{:S(2)}, u32[]{:S(2)}) %collective-permute-start.2) | collective-permute-done | bytes 1228832 | tf_op jit(solution)/shard_map/ppermute | solution.py:39
  65.2 2.5 collective-permute-start.4
  67.7 14.3 %collective-permute-done.3 = bf16[200,3,1024]{2,0,1:T(8,128)(2,1)S(1)} collective-permute-done((bf16[200,3,1024]{2,0,1:T(8,128)(2,1)S(1)}, bf16[200,3,1024]{2,0,1:T(8,128)(2,1)S(1)}, u32[]{:S(2)}, u32[]{:S(2)}) %collective-permute-start.3) | collective-permute-done | bytes 1228832 | tf_op jit(solution)/shard_map/ppermute | solution.py:44
  82.1 11.8 %collective-permute-done.4 = bf16[200,3,1024]{2,0,1:T(8,128)(2,1)S(1)} collective-permute-done((bf16[200,3,1024]{2,0,1:T(8,128)(2,1)}, bf16[200,3,1024]{2,0,1:T(8,128)(2,1)S(1)}, u32[]{:S(2)}, u32[]{:S(2)}) %collective-permute-start.4) | collective-permute-done | bytes 1228832 | tf_op jit(solution)/shard_map/ppermute | solution.py:39
  97.3 12.6 %collective-permute-done.5 = bf16[200,3,1024]{2,0,1:T(8,128)(2,1)} collective-permute-done((bf16[200,3,1024]{2,0,1:T(8,128)(2,1)S(1)}, bf16[200,3,1024]{2,0,1:T(8,128)(2,1)}, u32[]{:S(2)}, u32[]{:S(2)}) %collective-permute-start.5) | collective-permute-done | bytes 1228832 | tf_op jit(solution)/shard_map/ppermute | solution.py:44
  109.9 13.8 %collective-permute-done.6 = bf16[200,3,1024]{2,0,1:T(8,128)(2,1)} collective-permute-done((bf16[200,3,1024]{2,0,1:T(8,128)(2,1)S(1)}, bf16[200,3,1024]{2,0,1:T(8,128)(2,1)}, u32[]{:S(2)}, u32[]{:S(2)}) %collective-permute-start.6) | collective-permute-done | bytes 1228832 | tf_op jit(solution)/shard_map/ppermute | solution.py:39
  123.7 2.6 collective-permute-start.8
  126.3 14.9 %collective-permute-done.7 = bf16[200,3,1024]{2,0,1:T(8,128)(2,1)} collective-permute-done((bf16[200,3,1024]{2,0,1:T(8,128)(2,1)}, bf16[200,3,1024]{2,0,1:T(8,128)(2,1)}, u32[]{:S(2)}, u32[]{:S(2)}) %collective-permute-start.7) | collective-permute-done | bytes 1228832 | tf_op jit(solution)/shard_map/ppermute | solution.py:44
  141.2 14.5 %collective-permute-done.8 = bf16[200,3,1024]{2,0,1:T(8,128)(2,1)} collective-permute-done((bf16[200,3,1024]{2,0,1:T(8,128)(2,1)}, bf16[200,3,1024]{2,0,1:T(8,128)(2,1)}, u32[]{:S(2)}, u32[]{:S(2)}) %collective-permute-start.8) | collective-permute-done | bytes 1228832 | tf_op jit(solution)/shard_map/ppermute | solution.py:39
  158.2 19.1 %collective-permute-done.9 = bf16[200,3,1024]{2,0,1:T(8,128)(2,1)S(1)} collective-permute-done((bf16[200,3,1024]{2,0,1:T(8,128)(2,1)}, bf16[200,3,1024]{2,0,1:T(8,128)(2,1)S(1)}, u32[]{:S(2)}, u32[]{:S(2)}) %collective-permute-start.9) | collective-permute-done | bytes 1228832 | tf_op jit(solution)/shard_map/ppermute | solution.py:44
  178.4 24.5 %collective-permute-done.10 = bf16[200,3,1024]{2,0,1:T(8,128)(2,1)S(1)} collective-permute-done((bf16[200,3,1024]{2,0,1:T(8,128)(2,1)}, bf16[200,3,1024]{2,0,1:T(8,128)(2,1)S(1)}, u32[]{:S(2)}, u32[]{:S(2)}) %collective-permute-start.10) | collective-permute-done | bytes 1228832 | tf_op jit(solution)/shard_map/ppermute | solution.py:39
  205.3 7.9 collective-permute-done.11
  213.2 18.8 %collective-permute-done.12 = bf16[200,3,1024]{2,0,1:T(8,128)(2,1)} collective-permute-done((bf16[200,3,1024]{2,0,1:T(8,128)(2,1)S(1)}, bf16[200,3,1024]{2,0,1:T(8,128)(2,1)}, u32[]{:S(2)}, u32[]{:S(2)}) %collective-permute-start.12) | collective-permute-done | bytes 1228832 | tf_op jit(solution)/shard_map/ppermute | solution.py:39
  232.0 2.6 collective-permute-start.14
  237.8 4.1 all-reduce
  242.0 6.9 broadcast_in_dim.19
  248.9 16.6 %dynamic_update_slice.48 = bf16[3200,3,1024]{0,2,1:T(8,128)(2,1)} dynamic-update-slice(bf16[3200,3,1024]{0,2,1:T(8,128)(2,1)} %broadcast_in_dim.19, bf16[200,3,1024]{0,2,1:T(8,128)(2,1)S(1)} %copy.27, s32[]{:T(128)S(6)} %select_n.142, s32[]{:T(128)} %constant.121.clone.1, s32[]{:T(128)} %constant.121.clone.1) | dynamic-update-slice | bytes 2457604 | tf_op jit(solution)/shard_map/dynamic_update_slice | solution.py:35
  268.3 14.8 %dynamic_update_slice.49 = bf16[3200,3,1024]{0,2,1:T(8,128)(2,1)} dynamic-update-slice(bf16[3200,3,1024]{0,2,1:T(8,128)(2,1)} %dynamic_update_slice.48, bf16[200,3,1024]{0,2,1:T(8,128)(2,1)S(1)} %copy.28, s32[]{:T(128)S(6)} %select_n.144, s32[]{:T(128)} %constant.121.clone.1, s32[]{:T(128)} %constant.121.clone.1) | dynamic-update-slice | bytes 2457604 | tf_op jit(solution)/shard_map/dynamic_update_slice | solution.py:40
  283.8 16.6 %dynamic_update_slice.50 = bf16[3200,3,1024]{0,2,1:T(8,128)(2,1)} dynamic-update-slice(bf16[3200,3,1024]{0,2,1:T(8,128)(2,1)} %dynamic_update_slice.49, bf16[200,3,1024]{0,2,1:T(8,128)(2,1)S(1)} %copy.29, s32[]{:T(128)S(6)} %select_n.146, s32[]{:T(128)} %constant.121.clone.1, s32[]{:T(128)} %constant.121.clone.1) | dynamic-update-slice | bytes 2457604 | tf_op jit(solution)/shard_map/dynamic_update_slice | solution.py:45
  302.2 15.9 %dynamic_update_slice.51 = bf16[3200,3,1024]{0,2,1:T(8,128)(2,1)} dynamic-update-slice(bf16[3200,3,1024]{0,2,1:T(8,128)(2,1)} %dynamic_update_slice.50, bf16[200,3,1024]{0,2,1:T(8,128)(2,1)S(1)} %copy.30, s32[]{:T(128)S(6)} %select_n.148, s32[]{:T(128)} %constant.121.clone.1, s32[]{:T(128)} %constant.121.clone.1) | dynamic-update-slice | bytes 2457604 | tf_op jit(solution)/shard_map/dynamic_update_slice | solution.py:40
  318.7 16.8 %dynamic_update_slice.52 = bf16[3200,3,1024]{0,2,1:T(8,128)(2,1)} dynamic-update-slice(bf16[3200,3,1024]{0,2,1:T(8,128)(2,1)} %dynamic_update_slice.51, bf16[200,3,1024]{0,2,1:T(8,128)(2,1)S(1)} %copy.31, s32[]{:T(128)S(6)} %select_n.150, s32[]{:T(128)} %constant.121.clone.1, s32[]{:T(128)} %constant.121.clone.1) | dynamic-update-slice | bytes 2457604 | tf_op jit(solution)/shard_map/dynamic_update_slice | solution.py:45
  335.5 2.7 fusion.4
  338.8 16.7 %dynamic_update_slice.53 = bf16[3200,3,1024]{0,2,1:T(8,128)(2,1)} dynamic-update-slice(bf16[3200,3,1024]{0,2,1:T(8,128)(2,1)} %dynamic_update_slice.52, bf16[200,3,1024]{0,2,1:T(8,128)(2,1)S(1)} %copy.32, s32[]{:T(128)S(6)} %select_n.152, s32[]{:T(128)} %constant.121.clone.1, s32[]{:T(128)} %constant.121.clone.1) | dynamic-update-slice | bytes 2457604 | tf_op jit(solution)/shard_map/dynamic_update_slice | solution.py:40
  357.2 16.6 %dynamic_update_slice.54 = bf16[3200,3,1024]{0,2,1:T(8,128)(2,1)} dynamic-update-slice(bf16[3200,3,1024]{0,2,1:T(8,128)(2,1)} %dynamic_update_slice.53, bf16[200,3,1024]{0,2,1:T(8,128)(2,1)S(1)} %copy.33, s32[]{:T(128)S(6)} %select_n.154, s32[]{:T(128)} %constant.121.clone.1, s32[]{:T(128)} %constant.121.clone.1) | dynamic-update-slice | bytes 2457604 | tf_op jit(solution)/shard_map/dynamic_update_slice | solution.py:45
  375.4 16.7 %dynamic_update_slice.55 = bf16[3200,3,1024]{0,2,1:T(8,128)(2,1)} dynamic-update-slice(bf16[3200,3,1024]{0,2,1:T(8,128)(2,1)} %dynamic_update_slice.54, bf16[200,3,1024]{0,2,1:T(8,128)(2,1)S(1)} %copy.34, s32[]{:T(128)S(6)} %select_n.156, s32[]{:T(128)} %constant.121.clone.1, s32[]{:T(128)} %constant.121.clone.1) | dynamic-update-slice | bytes 2457604 | tf_op jit(solution)/shard_map/dynamic_update_slice | solution.py:40
  393.7 16.7 %dynamic_update_slice.56 = bf16[3200,3,1024]{0,2,1:T(8,128)(2,1)} dynamic-update-slice(bf16[3200,3,1024]{0,2,1:T(8,128)(2,1)} %dynamic_update_slice.55, bf16[200,3,1024]{0,2,1:T(8,128)(2,1)S(1)} %copy.35, s32[]{:T(128)S(6)} %select_n.158, s32[]{:T(128)} %constant.121.clone.1, s32[]{:T(128)} %constant.121.clone.1) | dynamic-update-slice | bytes 2457604 | tf_op jit(solution)/shard_map/dynamic_update_slice | solution.py:45
  412.2 16.6 %dynamic_update_slice.57 = bf16[3200,3,1024]{0,2,1:T(8,128)(2,1)} dynamic-update-slice(bf16[3200,3,1024]{0,2,1:T(8,128)(2,1)} %dynamic_update_slice.56, bf16[200,3,1024]{0,2,1:T(8,128)(2,1)S(1)} %copy.36, s32[]{:T(128)S(6)} %select_n.160, s32[]{:T(128)} %constant.121.clone.1, s32[]{:T(128)} %constant.121.clone.1) | dynamic-update-slice | bytes 2457604 | tf_op jit(solution)/shard_map/dynamic_update_slice | solution.py:40
  429.5 16.7 %dynamic_update_slice.58 = bf16[3200,3,1024]{0,2,1:T(8,128)(2,1)} dynamic-update-slice(bf16[3200,3,1024]{0,2,1:T(8,128)(2,1)} %dynamic_update_slice.57, bf16[200,3,1024]{0,2,1:T(8,128)(2,1)S(1)} %copy.37, s32[]{:T(128)S(6)} %select_n.162, s32[]{:T(128)} %constant.121.clone.1, s32[]{:T(128)} %constant.121.clone.1) | dynamic-update-slice | bytes 2457604 | tf_op jit(solution)/shard_map/dynamic_update_slice | solution.py:45
  446.9 16.6 %dynamic_update_slice.59 = bf16[3200,3,1024]{0,2,1:T(8,128)(2,1)} dynamic-update-slice(bf16[3200,3,1024]{0,2,1:T(8,128)(2,1)} %dynamic_update_slice.58, bf16[200,3,1024]{0,2,1:T(8,128)(2,1)S(1)} %copy.38, s32[]{:T(128)S(6)} %select_n.164, s32[]{:T(128)} %constant.121.clone.1, s32[]{:T(128)} %constant.121.clone.1) | dynamic-update-slice | bytes 2457604 | tf_op jit(solution)/shard_map/dynamic_update_slice | solution.py:40
  465.2 16.7 %dynamic_update_slice.60 = bf16[3200,3,1024]{0,2,1:T(8,128)(2,1)} dynamic-update-slice(bf16[3200,3,1024]{0,2,1:T(8,128)(2,1)} %dynamic_update_slice.59, bf16[200,3,1024]{0,2,1:T(8,128)(2,1)S(1)} %copy.39, s32[]{:T(128)S(6)} %select_n.166, s32[]{:T(128)} %constant.121.clone.1, s32[]{:T(128)} %constant.121.clone.1) | dynamic-update-slice | bytes 2457604 | tf_op jit(solution)/shard_map/dynamic_update_slice | solution.py:45
  483.5 16.6 %dynamic_update_slice.61 = bf16[3200,3,1024]{0,2,1:T(8,128)(2,1)} dynamic-update-slice(bf16[3200,3,1024]{0,2,1:T(8,128)(2,1)} %dynamic_update_slice.60, bf16[200,3,1024]{0,2,1:T(8,128)(2,1)S(1)} %copy.40, s32[]{:T(128)S(6)} %select_n.168, s32[]{:T(128)} %constant.121.clone.1, s32[]{:T(128)} %constant.121.clone.1) | dynamic-update-slice | bytes 2457604 | tf_op jit(solution)/shard_map/dynamic_update_slice | solution.py:40
  501.8 16.7 %dynamic_update_slice.62 = bf16[3200,3,1024]{0,2,1:T(8,128)(2,1)} dynamic-update-slice(bf16[3200,3,1024]{0,2,1:T(8,128)(2,1)} %dynamic_update_slice.61, bf16[200,3,1024]{0,2,1:T(8,128)(2,1)S(1)} %copy.41, s32[]{:T(128)S(6)} %select_n.170, s32[]{:T(128)} %constant.121.clone.1, s32[]{:T(128)} %constant.121.clone.1) | dynamic-update-slice | bytes 2457604 | tf_op jit(solution)/shard_map/dynamic_update_slice | solution.py:45
  520.6 16.6 %dynamic_update_slice.63 = bf16[3200,3,1024]{0,2,1:T(8,128)(2,1)} dynamic-update-slice(bf16[3200,3,1024]{0,2,1:T(8,128)(2,1)} %dynamic_update_slice.62, bf16[200,3,1024]{0,2,1:T(8,128)(2,1)S(1)} %copy.42, s32[]{:T(128)S(6)} %select_n.172, s32[]{:T(128)} %constant.121.clone.1, s32[]{:T(128)} %constant.121.clone.1) | dynamic-update-slice | bytes 2457604 | tf_op jit(solution)/shard_map/dynamic_update_slice | solution.py:40
  537.2 18.8 %fusion.1 = f32[512,3,1024]{2,0,1:T(8,128)} fusion(bf16[3200,3,1024]{0,2,1:T(8,128)(2,1)} %dynamic_update_slice.63, bf16[512,3200]{0,1:T(8,128)(2,1)} %all-gather.4.cloned.1.call-done, f32[3200]{0:T(1024)S(1)} %mul.184, f32[512]{0:T(512)S(1)} %add_rsqrt_fusion.2), kind=kOutput, calls=%fused_computation.2 | convolution fusion | flops 10072883200 | bytes 29243904 | tf_op jit(solution)/shard_map/dot_general | solution.py:49
  557.8 4.5 slice_bitcast_fusion
  564.6 3.8 all-reduce.1
  571.3 2.9 collective-permute-start.15
  581.0 5.5 fusion.23
  586.5 15.4 %fusion.44 = (f32[8,512]{1,0:T(8,128)S(1)}, f32[8,512,640]{2,1,0:T(8,128)}) fusion(f32[8,512,640]{2,1,0:T(8,128)} %fusion.23, pred[512,640]{1,0:T(8,128)(4,1)S(1)} %copy-done.15), kind=kOutput, calls=%fused_computation.76 | output fusion | flops 15729279 | bytes 21315584 | tf_op jit(solution)/shard_map/sub | solution.py:83
  601.9 5.9 fusion.19
  607.9 7.8 convolution_convert_fusion
  618.1 41.1 %reduce-scatter.2.cloned.1.call-done = bf16[512,1600]{0,1:T(8,128)(2,1)} async-done(((bf16[512,3200]{0,1:T(8,128)(2,1)}), bf16[512,1600]{0,1:T(8,128)(2,1)}) %reduce-scatter.2.cloned.1.call-update) | async-done | bytes 1638416 | tf_op jit(solution)/shard_map/reduce_scatter | solution.py:92
  663.9 60.7 %scatter_fusion = bf16[16,64,1600]{2,1,0:T(8,128)(2,1)S(1)} fusion(bf16[16,64,1600]{2,1,0:T(8,128)(2,1)S(1)} %broadcast_in_dim.18, s32[512]{0:T(512)S(1)} %bitcast.64, bf16[512,1600]{1,0:T(8,128)(2,1)} %copy.50), kind=kCustom, calls=%fused_computation | custom fusion | bytes 4919296 | tf_op jit(solution)/shard_map/scatter | solution.py:103
  724.6 82.8 %all_to_all.5 = bf16[16,64,1600]{2,1,0:T(8,128)(2,1)S(1)} all-to-all(bf16[16,64,1600]{2,1,0:T(8,128)(2,1)S(1)} %scatter_fusion), channel_id=1, replica_groups=mesh['group'=16,'tp'=2] {'group'}, dimensions={0} | all-to-all | bytes 6553600 | tf_op jit(solution)/shard_map/all_to_all | solution.py:105
  (121 shorter events, 56.0 us)
Async XLA Ops:
  6.5 228.8 %copy-start.3 = (bf16[200,3,1024]{2,0,1:T(8,128)(2,1)S(1)}, bf16[200,3,1024]{2,0,1:T(8,128)(2,1)}, u32[]{:S(2)}) copy-start(bf16[200,3,1024]{2,0,1:T(8,128)(2,1)} %param.10) | copy-start | bytes 3686404
  6.5 229.7 %copy-start.22 = (u32[32]{0:T(128)S(1)}, u32[32]{0:T(128)}, u32[]{:S(2)}) copy-start(u32[32]{0:T(128)} %constant.171) | copy-start | bytes 388
  6.5 231.0 %copy-start.21 = (bf16[1600]{0:T(1024)(128)(2,1)S(1)}, bf16[1600]{0:T(1024)(128)(2,1)}, u32[]{:S(2)}) copy-start(bf16[1600]{0:T(1024)(128)(2,1)} %param.9) | copy-start | bytes 9604
  6.5 235.4 %copy-start.20 = (f32[2,1024]{1,0:T(2,128)S(1)}, f32[2,1024]{1,0:T(2,128)}, u32[]{:S(2)}) copy-start(f32[2,1024]{1,0:T(2,128)} %param.11) | copy-start | bytes 24580
  6.5 328.9 %all-gather.4.cloned.1.call-start = ((), (), s32[]{:S(2)}) async-start(), calls=%async_computation.2 | async-start | bytes 4915200 | tf_op jit(solution)/shard_map/all_gather | solution.py:25
  6.6 29.8 %collective-permute-start = (bf16[200,3,1024]{2,0,1:T(8,128)(2,1)}, bf16[200,3,1024]{2,0,1:T(8,128)(2,1)}, u32[]{:S(2)}, u32[]{:S(2)}) collective-permute-start(bf16[200,3,1024]{2,0,1:T(8,128)(2,1)} %param.10), channel_id=1, source_target_pairs={{0,2},{2,4},{4,6},{6,8},{8,10},{10,12},{12,14},{14,16},{16,18},{18... | collective-permute-start | bytes 3686408 | tf_op jit(solution)/shard_map/ppermute | solution.py:39
  9.3 43.1 %collective-permute-start.1 = (bf16[200,3,1024]{2,0,1:T(8,128)(2,1)}, bf16[200,3,1024]{2,0,1:T(8,128)(2,1)S(1)}, u32[]{:S(2)}, u32[]{:S(2)}) collective-permute-start(bf16[200,3,1024]{2,0,1:T(8,128)(2,1)} %param.10), channel_id=1, source_target_pairs={{0,30},{2,0},{4,2},{6,4},{8,6},{10,8},{12,10},{14,12},{16,14},{18,... | collective-permute-start | bytes 3686408 | tf_op jit(solution)/shard_map/ppermute | solution.py:44
  36.4 28.8 %collective-permute-start.2 = (bf16[200,3,1024]{2,0,1:T(8,128)(2,1)}, bf16[200,3,1024]{2,0,1:T(8,128)(2,1)}, u32[]{:S(2)}, u32[]{:S(2)}) collective-permute-start(bf16[200,3,1024]{2,0,1:T(8,128)(2,1)} %collective-permute-done), channel_id=1, source_target_pairs={{0,2},{2,4},{4,6},{6,8},{8,10},{10,12},{12,14},{14,16},{16,18},{18... | collective-permute-start | bytes 3686408 | tf_op jit(solution)/shard_map/ppermute | solution.py:39
  38.9 569.0 %all-gather.6.cloned.1.call-start = ((), (), s32[]{:S(2)}) async-start(), calls=%async_computation.3 | async-start | bytes 6963200 | tf_op jit(solution)/shard_map/all_gather | solution.py:89
  52.4 183.0 %copy-start.4 = (bf16[200,3,1024]{2,0,1:T(8,128)(2,1)}, bf16[200,3,1024]{2,0,1:T(8,128)(2,1)S(1)}, u32[]{:S(2)}) copy-start(bf16[200,3,1024]{2,0,1:T(8,128)(2,1)S(1)} %collective-permute-done.1) | copy-start | bytes 3686404
  52.4 29.7 %collective-permute-start.3 = (bf16[200,3,1024]{2,0,1:T(8,128)(2,1)S(1)}, bf16[200,3,1024]{2,0,1:T(8,128)(2,1)S(1)}, u32[]{:S(2)}, u32[]{:S(2)}) collective-permute-start(bf16[200,3,1024]{2,0,1:T(8,128)(2,1)S(1)} %collective-permute-done.1), channel_id=1, source_target_pairs={{0,30},{2,0},{4,2},{6,4},{8,6},{10,8},{12,10},{14,12},{16,14},{18,... | collective-permute-start | bytes 3686408 | tf_op jit(solution)/shard_map/ppermute | solution.py:44
  65.2 28.7 %collective-permute-start.4 = (bf16[200,3,1024]{2,0,1:T(8,128)(2,1)}, bf16[200,3,1024]{2,0,1:T(8,128)(2,1)S(1)}, u32[]{:S(2)}, u32[]{:S(2)}) collective-permute-start(bf16[200,3,1024]{2,0,1:T(8,128)(2,1)} %collective-permute-done.2), channel_id=1, source_target_pairs={{0,2},{2,4},{4,6},{6,8},{8,10},{10,12},{12,14},{14,16},{16,18},{18... | collective-permute-start | bytes 3686408 | tf_op jit(solution)/shard_map/ppermute | solution.py:39
  82.0 41.6 %copy-start.8 = (bf16[200,3,1024]{2,0,1:T(8,128)(2,1)}, bf16[200,3,1024]{2,0,1:T(8,128)(2,1)S(1)}, u32[]{:S(2)}) copy-start(bf16[200,3,1024]{2,0,1:T(8,128)(2,1)S(1)} %collective-permute-done.3) | copy-start | bytes 3686404
  82.0 27.9 %collective-permute-start.5 = (bf16[200,3,1024]{2,0,1:T(8,128)(2,1)S(1)}, bf16[200,3,1024]{2,0,1:T(8,128)(2,1)}, u32[]{:S(2)}, u32[]{:S(2)}) collective-permute-start(bf16[200,3,1024]{2,0,1:T(8,128)(2,1)S(1)} %collective-permute-done.3), channel_id=1, source_target_pairs={{0,30},{2,0},{4,2},{6,4},{8,6},{10,8},{12,10},{14,12},{16,14},{18,... | collective-permute-start | bytes 3686408 | tf_op jit(solution)/shard_map/ppermute | solution.py:44
  93.9 1.0 copy-start.6
  94.9 28.8 %collective-permute-start.6 = (bf16[200,3,1024]{2,0,1:T(8,128)(2,1)S(1)}, bf16[200,3,1024]{2,0,1:T(8,128)(2,1)}, u32[]{:S(2)}, u32[]{:S(2)}) collective-permute-start(bf16[200,3,1024]{2,0,1:T(8,128)(2,1)S(1)} %collective-permute-done.4), channel_id=1, source_target_pairs={{0,2},{2,4},{4,6},{6,8},{8,10},{10,12},{12,14},{14,16},{16,18},{18... | collective-permute-start | bytes 3686408 | tf_op jit(solution)/shard_map/ppermute | solution.py:39
  109.9 31.3 %collective-permute-start.7 = (bf16[200,3,1024]{2,0,1:T(8,128)(2,1)}, bf16[200,3,1024]{2,0,1:T(8,128)(2,1)}, u32[]{:S(2)}, u32[]{:S(2)}) collective-permute-start(bf16[200,3,1024]{2,0,1:T(8,128)(2,1)} %collective-permute-done.5), channel_id=1, source_target_pairs={{0,30},{2,0},{4,2},{6,4},{8,6},{10,8},{12,10},{14,12},{16,14},{18,... | collective-permute-start | bytes 3686408 | tf_op jit(solution)/shard_map/ppermute | solution.py:44
  123.7 32.0 %collective-permute-start.8 = (bf16[200,3,1024]{2,0,1:T(8,128)(2,1)}, bf16[200,3,1024]{2,0,1:T(8,128)(2,1)}, u32[]{:S(2)}, u32[]{:S(2)}) collective-permute-start(bf16[200,3,1024]{2,0,1:T(8,128)(2,1)} %collective-permute-done.6), channel_id=1, source_target_pairs={{0,2},{2,4},{4,6},{6,8},{8,10},{10,12},{12,14},{14,16},{16,18},{18... | collective-permute-start | bytes 3686408 | tf_op jit(solution)/shard_map/ppermute | solution.py:39
  126.3 532.9 %reduce-scatter.2.cloned.1.call-start = ((), (), s32[]{:S(2)}) async-start(), calls=%async_computation.4 | async-start | bytes 4915200 | tf_op jit(solution)/shard_map/reduce_scatter | solution.py:92
  141.2 36.1 %collective-permute-start.9 = (bf16[200,3,1024]{2,0,1:T(8,128)(2,1)}, bf16[200,3,1024]{2,0,1:T(8,128)(2,1)S(1)}, u32[]{:S(2)}, u32[]{:S(2)}) collective-permute-start(bf16[200,3,1024]{2,0,1:T(8,128)(2,1)} %collective-permute-done.7), channel_id=1, source_target_pairs={{0,30},{2,0},{4,2},{6,4},{8,6},{10,8},{12,10},{14,12},{16,14},{18,... | collective-permute-start | bytes 3686408 | tf_op jit(solution)/shard_map/ppermute | solution.py:44
  155.7 47.2 %collective-permute-start.10 = (bf16[200,3,1024]{2,0,1:T(8,128)(2,1)}, bf16[200,3,1024]{2,0,1:T(8,128)(2,1)S(1)}, u32[]{:S(2)}, u32[]{:S(2)}) collective-permute-start(bf16[200,3,1024]{2,0,1:T(8,128)(2,1)} %collective-permute-done.8), channel_id=1, source_target_pairs={{0,2},{2,4},{4,6},{6,8},{8,10},{10,12},{12,14},{14,16},{16,18},{18... | collective-permute-start | bytes 3686408 | tf_op jit(solution)/shard_map/ppermute | solution.py:39
  177.3 1.0 copy-start.10
  178.4 34.8 %collective-permute-start.11 = (bf16[200,3,1024]{2,0,1:T(8,128)(2,1)S(1)}, bf16[200,3,1024]{2,0,1:T(8,128)(2,1)}, u32[]{:S(2)}, u32[]{:S(2)}) collective-permute-start(bf16[200,3,1024]{2,0,1:T(8,128)(2,1)S(1)} %collective-permute-done.9), channel_id=1, source_target_pairs={{0,30},{2,0},{4,2},{6,4},{8,6},{10,8},{12,10},{14,12},{16,14},{18,... | collective-permute-start | bytes 3686408 | tf_op jit(solution)/shard_map/ppermute | solution.py:44
  202.9 10.2 %copy-start.12 = (bf16[200,3,1024]{2,0,1:T(8,128)(2,1)}, bf16[200,3,1024]{2,0,1:T(8,128)(2,1)S(1)}, u32[]{:S(2)}) copy-start(bf16[200,3,1024]{2,0,1:T(8,128)(2,1)S(1)} %collective-permute-done.10) | copy-start | bytes 3686404
  202.9 29.1 %collective-permute-start.12 = (bf16[200,3,1024]{2,0,1:T(8,128)(2,1)S(1)}, bf16[200,3,1024]{2,0,1:T(8,128)(2,1)}, u32[]{:S(2)}, u32[]{:S(2)}) collective-permute-start(bf16[200,3,1024]{2,0,1:T(8,128)(2,1)S(1)} %collective-permute-done.10), channel_id=1, source_target_pairs={{0,2},{2,4},{4,6},{6,8},{8,10},{10,12},{12,14},{14,16},{16,18},{18... | collective-permute-start | bytes 3686408 | tf_op jit(solution)/shard_map/ppermute | solution.py:39
  213.2 287.0 %collective-permute-start.13 = (bf16[200,3,1024]{2,0,1:T(8,128)(2,1)}, bf16[200,3,1024]{2,0,1:T(8,128)(2,1)}, u32[]{:S(2)}, u32[]{:S(2)}) collective-permute-start(bf16[200,3,1024]{2,0,1:T(8,128)(2,1)} %collective-permute-done.11), channel_id=1, source_target_pairs={{0,30},{2,0},{4,2},{6,4},{8,6},{10,8},{12,10},{14,12},{16,14},{18,... | collective-permute-start | bytes 3686408 | tf_op jit(solution)/shard_map/ppermute | solution.py:44
  232.0 286.5 %collective-permute-start.14 = (bf16[200,3,1024]{2,0,1:T(8,128)(2,1)}, bf16[200,3,1024]{2,0,1:T(8,128)(2,1)}, u32[]{:S(2)}, u32[]{:S(2)}) collective-permute-start(bf16[200,3,1024]{2,0,1:T(8,128)(2,1)} %collective-permute-done.12), channel_id=1, source_target_pairs={{0,2},{2,4},{4,6},{6,8},{8,10},{10,12},{12,14},{14,16},{16,18},{18... | collective-permute-start | bytes 3686408 | tf_op jit(solution)/shard_map/ppermute | solution.py:39
  235.3 30.2 %collective-permute-start.16 = (s32[128]{0:T(128)S(1)}, s32[128]{0:T(128)S(1)}, u32[]{:S(2)}, u32[]{:S(2)}) collective-permute-start(s32[128]{0:T(128)S(1)} %dynamic_slice.11), channel_id=1, source_target_pairs={{0,2},{2,0},{4,6},{6,4},{8,10},{10,8},{12,14},{14,12},{16,18},{18,... | collective-permute-start | bytes 1544 | tf_op jit(solution)/shard_map/ppermute | solution.py:14
  248.9 16.6 %copy-start.19 = (s32[512]{0:T(512)S(1)}, s32[512]{0:T(512)}, u32[]{:S(2)}) copy-start(s32[512]{0:T(512)} %param.14) | copy-start | bytes 6148
  266.5 16.6 %copy-start.5 = (bf16[200,3,1024]{2,0,1:T(8,128)(2,1)S(1)}, bf16[200,3,1024]{2,0,1:T(8,128)(2,1)}, u32[]{:S(2)}) copy-start(bf16[200,3,1024]{2,0,1:T(8,128)(2,1)} %copy-done.4) | copy-start | bytes 3686404
  300.4 17.6 %copy-start.9 = (bf16[200,3,1024]{2,0,1:T(8,128)(2,1)S(1)}, bf16[200,3,1024]{2,0,1:T(8,128)(2,1)}, u32[]{:S(2)}) copy-start(bf16[200,3,1024]{2,0,1:T(8,128)(2,1)} %copy-done.8) | copy-start | bytes 3686404
  318.7 19.5 %copy-start.7 = (bf16[200,3,1024]{2,0,1:T(8,128)(2,1)S(1)}, bf16[200,3,1024]{2,0,1:T(8,128)(2,1)}, u32[]{:S(2)}) copy-start(bf16[200,3,1024]{2,0,1:T(8,128)(2,1)} %copy-done.6) | copy-start | bytes 3686404
  410.4 18.4 %copy-start.11 = (bf16[200,3,1024]{2,0,1:T(8,128)(2,1)S(1)}, bf16[200,3,1024]{2,0,1:T(8,128)(2,1)}, u32[]{:S(2)}) copy-start(bf16[200,3,1024]{2,0,1:T(8,128)(2,1)} %copy-done.10) | copy-start | bytes 3686404
  429.5 16.7 %copy-start.13 = (bf16[200,3,1024]{2,0,1:T(8,128)(2,1)S(1)}, bf16[200,3,1024]{2,0,1:T(8,128)(2,1)}, u32[]{:S(2)}) copy-start(bf16[200,3,1024]{2,0,1:T(8,128)(2,1)} %copy-done.12) | copy-start | bytes 3686404
  569.9 4.3 copy-start
  571.3 5.2 collective-permute-start.15
  576.5 4.5 copy-start.1
  581.0 5.5 copy-start.15
  586.5 15.4 %copy-start.14 = (bf16[512,1,1024]{0,2,1:T(8,128)(2,1)S(1)}, bf16[512,1,1024]{0,2,1:T(8,128)(2,1)}, u32[]{:S(2)}) copy-start(bf16[512,1,1024]{0,2,1:T(8,128)(2,1)} %copy.53) | copy-start | bytes 3145732
  586.5 15.4 %copy-start.16 = (bf16[1,128,1024]{1,2,0:T(8,128)(2,1)S(1)}, bf16[1,128,1024]{1,2,0:T(8,128)(2,1)}, u32[]{:S(2)}) copy-start(bf16[1,128,1024]{1,2,0:T(8,128)(2,1)} %copy.44) | copy-start | bytes 786436
  615.7 0.7 copy-start.17
  615.7 43.5 %copy-start.2 = (bf16[512,1600]{0,1:T(8,128)(2,1)S(1)}, bf16[512,1600]{0,1:T(8,128)(2,1)}, u32[]{:S(2)}) copy-start(bf16[512,1600]{0,1:T(8,128)(2,1)} %param.8) | copy-start | bytes 4915204
  615.7 43.5 %copy-start.18 = (f32[1600]{0:T(1024)S(1)}, f32[1600]{0:T(1024)}, u32[]{:S(2)}) copy-start(f32[1600]{0:T(1024)} %param.13) | copy-start | bytes 19204
Sparse Core Ops, SparseCore 0:
  39.0 46.1 all-gather.3
  126.4 92.2 all-gather.5
  615.8 43.3 reduce-scatter.1
